TPU v7x, 32 devices: a whole 2x2x4 slice. The times are simulated.
32 devices in a mesh: clips: 2 (over y), frame: 4 (over z), rows: 2 (over x), view: 2 (over core).
Axes of the slice: x: 2, y: 2, z: 4, core: 2. Of those that a mesh axis runs over, the one named last changes fastest.
Arguments:
- feats: bfloat16 [4, 4, 8, 480, 256], P(('clips', 'view'), 'frame', 'rows'), parts along dimension 0, may hold values from -8 to 8
- norm_gains: float32 [3, 256], replicated, may hold values from 0.6 to 10
- cross_qkv: bfloat16 [256, 768], replicated, may hold values from -0.45 to 0.45
- cross_out: bfloat16 [256, 256], replicated, may hold values from -0.375 to 0.375
- time_qkv: bfloat16 [256, 768], replicated, may hold values from -0.45 to 0.45
- time_out: bfloat16 [256, 256], replicated, may hold values from -0.375 to 0.375
- mlp_in: bfloat16 [256, 1024], replicated, may hold values from -0.375 to 0.375
- mlp_out: bfloat16 [1024, 256], replicated, may hold values from -0.1875 to 0.1875
Outputs:
- result: bfloat16 [4, 4, 8, 480, 256], P(('clips', 'view'), 'frame', 'rows'), parts along dimension 0
There are 2 independent parts, one for each index of `clips`. A program takes and returns all parts, laid end to end along the dimension named above; an argument that names none is the same for every part. Nothing has to cross between parts.
All inputs are finite; a program needn't handle non-finite values.
Results may differ from a plain program's by a relative error of at most 0.012.
Values may be sent and summed in bfloat16 or wider, within the bound.
No kernel may reach another device: no remote copies, remote signals or barrier semaphores. Data moves between devices by JAX's collectives and lax.ppermute only.
A program may use at most 64 MiB of HBM per device.

v0:
```python
import jax
import jax.numpy as jnp
from jax import lax
from jax.sharding import PartitionSpec as P

HEADS = 8
EPSILON = 1e-05


def swapped(value, axis, bit):
    return lax.ppermute(value, axis, [(i, i ^ 1 << bit) for i in range(lax.axis_size(axis))])


def layer_norm(values, norm_gain):
    wide = values.astype(jnp.float32)
    centre = jnp.mean(wide, axis=-1, keepdims=True)
    spread = jnp.mean((wide - centre) ** 2, axis=-1, keepdims=True)
    return ((wide - centre) * lax.rsqrt(spread + EPSILON) * norm_gain).astype(jnp.bfloat16)


def row_attend(queries, key_rows, value_rows):
    length, channels = queries.shape
    head_dim = channels // HEADS
    q_heads = queries.reshape(length, HEADS, head_dim)
    k_heads = key_rows.reshape(length, HEADS, head_dim)
    v_heads = value_rows.reshape(length, HEADS, head_dim)
    scores = jnp.einsum(
        "qhd,khd->hqk", q_heads, k_heads, preferred_element_type=jnp.float32
    ) * head_dim ** (-0.5)
    top_score = jnp.max(scores, axis=-1, keepdims=True)
    expo = jnp.exp(scores - top_score)
    shares = (expo / jnp.sum(expo, axis=-1, keepdims=True)).astype(jnp.bfloat16)
    mixed = jnp.einsum("hqk,khd->qhd", shares, v_heads, preferred_element_type=jnp.float32)
    return mixed.reshape(length, channels).astype(jnp.bfloat16)


def time_attend(queries, key_rows, value_rows):
    frames, pixels, channels = queries.shape
    head_dim = channels // HEADS
    q_heads = queries.reshape(frames, pixels, HEADS, head_dim)
    k_heads = key_rows.reshape(frames, pixels, HEADS, head_dim)
    v_heads = value_rows.reshape(frames, pixels, HEADS, head_dim)
    scores = jnp.einsum(
        "fnhd,gnhd->hfgn", q_heads, k_heads, preferred_element_type=jnp.float32
    ) * head_dim ** (-0.5)
    top_score = jnp.max(scores, axis=2, keepdims=True)
    expo = jnp.exp(scores - top_score)
    shares = (expo / jnp.sum(expo, axis=2, keepdims=True)).astype(jnp.bfloat16)
    mixed = jnp.einsum("hfgn,gnhd->fnhd", shares, v_heads, preferred_element_type=jnp.float32)
    return mixed.reshape(frames, pixels, channels).astype(jnp.bfloat16)


def local(feats, norm_gains, cross_qkv, cross_out, time_qkv, time_out, mlp_in, mlp_out):
    rows_here, row_width, channels = (feats.shape[2], feats.shape[3], feats.shape[4])
    frame_count = lax.axis_size("frame")
    tokens_flat = feats[0, 0].reshape(-1, channels)
    pixel_count = tokens_flat.shape[0]
    block_pixels = pixel_count // frame_count
    normed_a = layer_norm(tokens_flat, norm_gains[0])
    projected = jnp.dot(normed_a, cross_qkv, preferred_element_type=jnp.float32).astype(
        jnp.bfloat16
    )
    queries = projected[:, :channels]
    partner = swapped(projected[:, channels:], "view", 0)

    def cross_row(pieces):
        return row_attend(pieces[0], pieces[1][:, :channels], pieces[1][:, channels:])

    cross_mix = lax.map(
        cross_row,
        (
            queries.reshape(rows_here, row_width, channels),
            partner.reshape(rows_here, row_width, 2 * channels),
        ),
    )
    cross_mix = cross_mix.reshape(-1, channels)
    stream_b = (
        tokens_flat.astype(jnp.float32)
        + jnp.dot(cross_mix, cross_out, preferred_element_type=jnp.float32)
    ).astype(jnp.bfloat16)
    normed_b = layer_norm(stream_b, norm_gains[1])
    outgoing = normed_b.reshape(1, frame_count, block_pixels, channels)
    gathered = lax.all_to_all(outgoing, "frame", split_axis=1, concat_axis=0, tiled=True)[:, 0]
    frames, pixels, _ = gathered.shape
    projected_b = jnp.dot(
        gathered.reshape(-1, channels), time_qkv, preferred_element_type=jnp.float32
    ).astype(jnp.bfloat16)
    projected_b = projected_b.reshape(frames, pixels, 3 * channels)
    mixed = time_attend(
        projected_b[..., :channels],
        projected_b[..., channels : 2 * channels],
        projected_b[..., 2 * channels :],
    )
    time_mix = mixed[:, None]
    returned = lax.all_to_all(time_mix, "frame", split_axis=0, concat_axis=1, tiled=True).reshape(
        pixel_count, channels
    )
    stream_c = (
        stream_b.astype(jnp.float32)
        + jnp.dot(returned, time_out, preferred_element_type=jnp.float32)
    ).astype(jnp.bfloat16)
    normed_c = layer_norm(stream_c, norm_gains[2])
    inner_act = jax.nn.gelu(
        jnp.dot(normed_c, mlp_in, preferred_element_type=jnp.float32), approximate=True
    ).astype(jnp.bfloat16)
    result = (
        stream_c.astype(jnp.float32)
        + jnp.dot(inner_act, mlp_out, preferred_element_type=jnp.float32)
    ).astype(jnp.bfloat16)
    return result.reshape(1, 1, rows_here, row_width, channels)


def solution(mesh):
    placed = (P(("clips", "view"), "frame", "rows", None, None), P(), P(), P(), P(), P(), P(), P())
    return jax.shard_map(
        local,
        mesh=mesh,
        in_specs=placed,
        out_specs=P(("clips", "view"), "frame", "rows", None, None),
        check_vma=False,
    )
```

profile of v0, /device:TPU:0, one launch (start us, length us, event | category | flops | bytes accessed | tf_op | source)
XLA Modules:
  0.0 185.9 jit_solution(15738146926986763434)
XLA Ops:
  0.0 1.6 convert_reduce_fusion.2
  1.7 1.8 multiply_reduce_fusion.1
  3.6 0.8 fusion.60
  4.5 1.8 fusion.42
  6.3 0.9 convolution_convert_fusion.2
  7.2 1.4 slice.40
  9.1 1.0 slice.41
  10.2 2.8 %collective-permute-done = bf16[1920,512]{1,0:T(8,128)(2,1)S(1)} collective-permute-done((bf16[1920,512]{1,0:T(8,128)(2,1)}, bf16[1920,512]{1,0:T(8,128)(2,1)S(1)}, u32[]{:S(2)}, u32[]{:S(2)}) %collective-permute-start) | collective-permute-done | bytes 1966112 | tf_op jit(solution)/shard_map/ppermute | solution.py:11
  12.9 1.4 copy-done.2
  14.3 48.6 %while.10 = (s32[]{:T(128)}, bf16[4,480,256]{2,1,0:T(8,128)(2,1)}, bf16[4,480,512]{2,1,0:T(8,128)(2,1)}, bf16[4,480,256]{2,1,0:T(8,128)(2,1)}, s32[]{:T(128)}) while((s32[]{:T(128)}, bf16[4,480,256]{2,1,0:T(8,128)(2,1)}, bf16[4,480,512]{2,1,0:T(8,128)(2,1)}, bf16[4,480,256]{2,1,0:T(8,128)(2,1)}, s32[]{:T(128)}) %tuple.39), condition=%wide.region_5.6_spmd, body=%wide.region_2.5_spmd.sunk | while | flops 245268960 | bytes 20675140 | solution.py:69
  14.3 1.2 constant_dynamic-slice_fusion.4
  15.7 1.0 constant_dynamic-slice_fusion.5
  16.8 4.8 %fusion.91 = (f32[8,480]{1,0:T(8,128)S(1)}, f32[8,480,480]{1,2,0:T(8,128)}) fusion(bf16[480,8,32]{0,2,1:T(8,128)(2,1)S(1)} %bitcast.83, bf16[480,8,32]{0,2,1:T(8,128)(2,1)S(1)} %bitcast.86), kind=kOutput, calls=%fused_computation.73.clone.1 | convolution fusion | flops 123494880 | bytes 7879680 | tf_op jit(solution)/shard_map/while/body/eval_jaxpr/sub | solution.py:31
  21.6 4.0 %fusion.92 = bf16[8,32,480]{2,1,0:T(8,128)(2,1)S(1)} fusion(bf16[480,8,32]{0,2,1:T(8,128)(2,1)S(1)} %bitcast.85, f32[8,480,480]{1,2,0:T(8,128)} %get-tuple-element.101, f32[8,480]{1,0:T(8,128)S(1)} %get-tuple-element.102), kind=kOutput, calls=%fused_computation.7.clone.1 | convolution fusion | flops 121774080 | bytes 7879680 | tf_op jit(solution)/shard_map/while/body/eval_jaxpr/hqk,khd->qhd/dot_general | solution.py:33
  25.8 0.7 constant_dynamic-update-slice_fusion.2
  26.5 1.1 constant_dynamic-slice_fusion.4
  27.8 1.0 constant_dynamic-slice_fusion.5
  28.9 4.8 %fusion.91 = (f32[8,480]{1,0:T(8,128)S(1)}, f32[8,480,480]{1,2,0:T(8,128)}) fusion(bf16[480,8,32]{0,2,1:T(8,128)(2,1)S(1)} %bitcast.83, bf16[480,8,32]{0,2,1:T(8,128)(2,1)S(1)} %bitcast.86), kind=kOutput, calls=%fused_computation.73.clone.1 | convolution fusion | flops 123494880 | bytes 7879680 | tf_op jit(solution)/shard_map/while/body/eval_jaxpr/sub | solution.py:31
  33.7 4.0 %fusion.92 = bf16[8,32,480]{2,1,0:T(8,128)(2,1)S(1)} fusion(bf16[480,8,32]{0,2,1:T(8,128)(2,1)S(1)} %bitcast.85, f32[8,480,480]{1,2,0:T(8,128)} %get-tuple-element.101, f32[8,480]{1,0:T(8,128)S(1)} %get-tuple-element.102), kind=kOutput, calls=%fused_computation.7.clone.1 | convolution fusion | flops 121774080 | bytes 7879680 | tf_op jit(solution)/shard_map/while/body/eval_jaxpr/hqk,khd->qhd/dot_general | solution.py:33
  37.9 0.7 constant_dynamic-update-slice_fusion.2
  38.6 1.1 constant_dynamic-slice_fusion.4
  39.9 1.0 constant_dynamic-slice_fusion.5
  41.1 4.8 %fusion.91 = (f32[8,480]{1,0:T(8,128)S(1)}, f32[8,480,480]{1,2,0:T(8,128)}) fusion(bf16[480,8,32]{0,2,1:T(8,128)(2,1)S(1)} %bitcast.83, bf16[480,8,32]{0,2,1:T(8,128)(2,1)S(1)} %bitcast.86), kind=kOutput, calls=%fused_computation.73.clone.1 | convolution fusion | flops 123494880 | bytes 7879680 | tf_op jit(solution)/shard_map/while/body/eval_jaxpr/sub | solution.py:31
  45.9 4.0 %fusion.92 = bf16[8,32,480]{2,1,0:T(8,128)(2,1)S(1)} fusion(bf16[480,8,32]{0,2,1:T(8,128)(2,1)S(1)} %bitcast.85, f32[8,480,480]{1,2,0:T(8,128)} %get-tuple-element.101, f32[8,480]{1,0:T(8,128)S(1)} %get-tuple-element.102), kind=kOutput, calls=%fused_computation.7.clone.1 | convolution fusion | flops 121774080 | bytes 7879680 | tf_op jit(solution)/shard_map/while/body/eval_jaxpr/hqk,khd->qhd/dot_general | solution.py:33
  50.0 0.7 constant_dynamic-update-slice_fusion.2
  50.7 1.1 constant_dynamic-slice_fusion.4
  52.1 1.0 constant_dynamic-slice_fusion.5
  53.2 4.8 %fusion.91 = (f32[8,480]{1,0:T(8,128)S(1)}, f32[8,480,480]{1,2,0:T(8,128)}) fusion(bf16[480,8,32]{0,2,1:T(8,128)(2,1)S(1)} %bitcast.83, bf16[480,8,32]{0,2,1:T(8,128)(2,1)S(1)} %bitcast.86), kind=kOutput, calls=%fused_computation.73.clone.1 | convolution fusion | flops 123494880 | bytes 7879680 | tf_op jit(solution)/shard_map/while/body/eval_jaxpr/sub | solution.py:31
  58.0 4.0 %fusion.92 = bf16[8,32,480]{2,1,0:T(8,128)(2,1)S(1)} fusion(bf16[480,8,32]{0,2,1:T(8,128)(2,1)S(1)} %bitcast.85, f32[8,480,480]{1,2,0:T(8,128)} %get-tuple-element.101, f32[8,480]{1,0:T(8,128)S(1)} %get-tuple-element.102), kind=kOutput, calls=%fused_computation.7.clone.1 | convolution fusion | flops 121774080 | bytes 7879680 | tf_op jit(solution)/shard_map/while/body/eval_jaxpr/hqk,khd->qhd/dot_general | solution.py:33
  62.1 0.7 constant_dynamic-update-slice_fusion.2
  62.9 1.8 convert_reduce_fusion.1
  64.7 0.6 fusion.37
  65.9 30.7 %all_to_all.8 = bf16[1,4,480,256]{3,2,0,1:T(8,128)(2,1)S(1)} all-to-all(bf16[1,4,480,256]{3,2,0,1:T(8,128)(2,1)S(1)} %bitcast.92), channel_id=1, replica_groups=mesh['clips'=2,'frame'=4,'rows'=2,'view'=2] {'frame'}, dimensions={1} | all-to-all | bytes 1966080 | tf_op jit(solution)/shard_map/all_to_all | solution.py:83
  96.6 0.9 convolution_convert_fusion.1
  97.5 1.5 fusion.59
  99.0 1.5 copy.73
  100.5 4.6 %copy.60 = bf16[4,480,8,32]{3,0,1,2:T(4,128)(2,1)} copy(bf16[4,480,8,32]{1,3,2,0:T(8,128)(2,1)S(1)} %bitcast.88) | data formatting | bytes 1966080 | tf_op jit(solution)/shard_map/reshape | solution.py:41
  105.0 1.5 copy.74
  106.5 4.5 %copy.61 = bf16[4,480,8,32]{3,0,1,2:T(4,128)(2,1)} copy(bf16[4,480,8,32]{1,3,2,0:T(8,128)(2,1)S(1)} %bitcast.89) | data formatting | bytes 1966080 | tf_op jit(solution)/shard_map/reshape | solution.py:40
  111.0 8.4 %fusion.61 = f32[8,480,4,4]{3,2,1,0:T(4,128)} fusion(bf16[4,480,8,32]{3,0,1,2:T(4,128)(2,1)} %copy.60, bf16[4,480,8,32]{3,0,1,2:T(4,128)(2,1)} %copy.61), kind=kOutput, calls=%fused_computation.76 | convolution fusion | flops 3932160 | bytes 2211840 | tf_op jit(solution)/shard_map/fnhd,gnhd->hfgn/dot_general | solution.py:43
  119.5 5.1 %copy.62 = f32[8,480,4,4]{1,0,2,3:T(8,128)S(1)} copy(f32[8,480,4,4]{3,2,1,0:T(4,128)} %fusion.61) | data formatting | bytes 491520 | tf_op jit(solution)/shard_map/fnhd,gnhd->hfgn/dot_general | solution.py:43
  124.7 7.4 %copy.64 = bf16[8,4,4,480]{2,1,0,3:T(4,128)(2,1)} copy(bf16[8,4,4,480]{3,0,2,1:T(8,128)(2,1)S(1)} %divide_convert_fusion.4) | data formatting | bytes 245760 | tf_op jit(solution)/shard_map/convert_element_type | solution.py:48
  132.7 4.7 %copy.63 = bf16[4,480,8,32]{3,0,2,1:T(4,128)(2,1)} copy(bf16[4,480,8,32]{1,3,2,0:T(8,128)(2,1)S(1)} %bitcast.90) | data formatting | bytes 1966080 | tf_op jit(solution)/shard_map/reshape | solution.py:42
  137.4 9.5 %fusion.20 = bf16[4,480,8,32]{3,0,2,1:T(4,128)(2,1)} fusion(bf16[4,480,8,32]{3,0,2,1:T(4,128)(2,1)} %copy.63, bf16[8,4,4,480]{2,1,0,3:T(4,128)(2,1)} %copy.64), kind=kOutput, calls=%fused_computation.24 | convolution fusion | flops 4423680 | bytes 2088960 | tf_op jit(solution)/shard_map/hfgn,gnhd->fnhd/dot_general | solution.py:49
  146.9 5.4 %copy.65 = bf16[4,480,8,32]{1,3,2,0:T(8,128)(2,1)S(1)} copy(bf16[4,480,8,32]{3,0,2,1:T(4,128)(2,1)} %fusion.20) | data formatting | bytes 1966080 | tf_op jit(solution)/shard_map/convert_element_type | solution.py:50
  152.9 26.7 %all_to_all.9 = bf16[4,1,480,256]{3,2,1,0:T(8,128)(2,1)S(1)} all-to-all(bf16[4,1,480,256]{3,2,1,0:T(8,128)(2,1)S(1)} %copy.66), channel_id=1, replica_groups=mesh['clips'=2,'frame'=4,'rows'=2,'view'=2] {'frame'}, dimensions={0} | all-to-all | bytes 1966080 | tf_op jit(solution)/shard_map/all_to_all | solution.py:95
  179.6 1.5 convert_reduce_fusion
  181.7 4.2 %fusion.27 = bf16[1920,256]{1,0:T(8,128)(2,1)} fusion(bf16[1024,256]{1,0:T(8,128)(2,1)S(1)} %copy-done, bf16[256,1024]{1,0:T(8,128)(2,1)S(1)} %copy-done.6, bf16[1920,256]{1,0:T(8,128)(2,1)S(1)} %get-tuple-element.69, f32[256]{0:T(256)S(1)} %bitcast.98, f32[1920]{0:T(1024)S(1)} %add_rsqrt_fusion, f32[1920]{0:T(1024)S(1)} %broadcast_multiply_fusion), kind=kOutput, calls=%fused_computation.37 | convolution fusion | flops 2034892800 | bytes 3031040 | tf_op jit(solution)/shard_map/dot_general | solution.py:108
  (46 shorter events, 5.2 us)
Async XLA Ops:
  0.0 181.7 %copy-start = (bf16[1024,256]{1,0:T(8,128)(2,1)S(1)}, bf16[1024,256]{1,0:T(8,128)(2,1)}, u32[]{:S(2)}) copy-start(bf16[1024,256]{1,0:T(8,128)(2,1)} %param.17) | copy-start | bytes 1572868
  0.0 6.2 %copy-start.3 = (bf16[256,768]{1,0:T(8,128)(2,1)S(1)}, bf16[256,768]{1,0:T(8,128)(2,1)}, u32[]{:S(2)}) copy-start(bf16[256,768]{1,0:T(8,128)(2,1)} %param.12) | copy-start | bytes 1179652
  8.6 4.3 %collective-permute-start = (bf16[1920,512]{1,0:T(8,128)(2,1)}, bf16[1920,512]{1,0:T(8,128)(2,1)S(1)}, u32[]{:S(2)}, u32[]{:S(2)}) collective-permute-start(bf16[1920,512]{1,0:T(8,128)(2,1)} %slice.40), channel_id=1, source_target_pairs={{0,1},{1,0},{2,3},{3,2},{4,5},{5,4},{6,7},{7,6},{8,9},{9,8},{10,11... | collective-permute-start | bytes 5898248 | tf_op jit(solution)/shard_map/ppermute | solution.py:11
  12.9 1.4 copy-start.2
  14.3 48.6 %copy-start.1 = (bf16[1,1,4,480,256]{4,3,2,1,0:T(8,128)(2,1)S(1)}, bf16[1,1,4,480,256]{4,3,2,1,0:T(8,128)(2,1)}, u32[]{:S(2)}) copy-start(bf16[1,1,4,480,256]{4,3,2,1,0:T(8,128)(2,1)} %param.10) | copy-start | bytes 2949124
  14.3 48.6 %copy-start.5 = (bf16[256,256]{1,0:T(8,128)(2,1)S(1)}, bf16[256,256]{1,0:T(8,128)(2,1)}, u32[]{:S(2)}) copy-start(bf16[256,256]{1,0:T(8,128)(2,1)} %param.13) | copy-start | bytes 393220
  62.9 33.7 %copy-start.4 = (bf16[256,768]{1,0:T(8,128)(2,1)S(1)}, bf16[256,768]{1,0:T(8,128)(2,1)}, u32[]{:S(2)}) copy-start(bf16[256,768]{1,0:T(8,128)(2,1)} %param.14) | copy-start | bytes 1179652
  179.6 2.1 %copy-start.6 = (bf16[256,1024]{1,0:T(8,128)(2,1)S(1)}, bf16[256,1024]{1,0:T(8,128)(2,1)}, u32[]{:S(2)}) copy-start(bf16[256,1024]{1,0:T(8,128)(2,1)} %param.16) | copy-start | bytes 1572868
where the time goes:
time: 187 us; the launch traced here: 186 us
  matrix products  62.5 us (33%)
  blocking collectives  57.4 us (31%)
  local copies, waits for them, and re-layouts  55.2 us (30%)
  other arithmetic  7.24 us (4%)
  waiting for transfers between devices  2.78 us (1%)
    all_to_all x1, blocking collectives, local(): lax.all_to_all(outgoing, 'frame', split_axis=1, concat_axis=0, tiled=True)  30.7 us
    all_to_all x1, blocking collectives, local(): lax.all_to_all(time_mix, 'frame', split_axis=0, concat_axis=1, tiled=True)  26.7 us
    sub x4, matrix products, row_attend(): expo = jnp.exp(scores - top_score)  19.1 us
    dot_general x4, matrix products, row_attend(): jnp.einsum('hqk,khd->qhd', shares, v_heads, preferred_element_type=jnp.fl...  16.1 us
    dynamic_slice x16, local copies, waits for them, and re-layouts, local(): lax.map(cross_row, (queries.reshape(rows_here, row_width, channels), part...  9.61 us
    dot_general x1, matrix products, time_attend(): jnp.einsum('hfgn,gnhd->fnhd', shares, v_heads, preferred_element_type=jnp...  9.5 us
    dot_general x1, matrix products, time_attend(): jnp.einsum('fnhd,gnhd->hfgn', q_heads, k_heads, preferred_element_type=jn...  8.41 us
    convert_element_type x1, local copies, waits for them, and re-layouts, time_attend(): shares = (expo / jnp.sum(expo, axis=2, keepdims=True)).astype(jnp.bfloat16)  7.42 us
  transfers between devices with their start and end apart: 1, of which 1 were waited for; matrix products, arithmetic and copies ran while one was open for 1% of the time, Pallas kernels for 0%

commit v1 on v0

--- a/solution.py
+++ b/solution.py
@@ -92,9 +92,12 @@
         projected_b[..., 2 * channels :],
     )
     time_mix = mixed[:, None]
-    returned = lax.all_to_all(time_mix, "frame", split_axis=0, concat_axis=1, tiled=True).reshape(
-        pixel_count, channels
-    )
+    returned = jnp.concatenate(
+        lax.all_to_all(
+            jnp.stack(jnp.split(time_mix, lax.axis_size("frame"), axis=0)), "frame", 0, 0
+        ),
+        axis=1,
+    ).reshape(pixel_count, channels)
     stream_c = (
         stream_b.astype(jnp.float32)
         + jnp.dot(returned, time_out, preferred_element_type=jnp.float32)

time: 187 us -> 215 us (1.15)
  local copies, waits for them, and re-layouts: 55.2 us -> 82.4 us
    split x0 -> x5, local copies, waits for them, and re-layouts: none -> 32.6 us  [local(): jnp.split(time_mix, lax.axis_size('frame'), axis=0)]
    convert_element_type x2 -> x0, local copies, waits for them, and re-layouts: 5.96 us -> none  [time_attend(): return mixed.reshape(frames, pixels, channels).astype(jnp.bfloat16)]
  transfers between devices with their start and end apart: 1 -> 1, of which waited for: 1 -> 1; matrix products, arithmetic and copies ran while one was open for 1% -> 0% of each run, Pallas kernels for 0% -> 0%
where the time goes in v1:
time: 215 us; the launch traced here: 214 us
  local copies, waits for them, and re-layouts  82.4 us (38%)
  matrix products  62.2 us (29%)
  blocking collectives  57.5 us (27%)
  other arithmetic  8.35 us (4%)
  waiting for transfers between devices  2.78 us (1%)
    split x5, local copies, waits for them, and re-layouts, local(): jnp.split(time_mix, lax.axis_size('frame'), axis=0)  32.6 us
    all_to_all x1, blocking collectives, local(): lax.all_to_all(outgoing, 'frame', split_axis=1, concat_axis=0, tiled=True)  30.7 us
    all_to_all x1, blocking collectives, local(): lax.all_to_all(jnp.stack(jnp.split(time_mix, lax.axis_size('frame'), axis...  26.9 us
    sub x4, matrix products, row_attend(): expo = jnp.exp(scores - top_score)  19.1 us
    dot_general x4, matrix products, row_attend(): jnp.einsum('hqk,khd->qhd', shares, v_heads, preferred_element_type=jnp.fl...  16.1 us
    dynamic_slice x16, local copies, waits for them, and re-layouts, local(): lax.map(cross_row, (queries.reshape(rows_here, row_width, channels), part...  9.61 us
    dot_general x1, matrix products, time_attend(): jnp.einsum('hfgn,gnhd->fnhd', shares, v_heads, preferred_element_type=jnp...  9.4 us
    dot_general x1, matrix products, time_attend(): jnp.einsum('fnhd,gnhd->hfgn', q_heads, k_heads, preferred_element_type=jn...  8.41 us
  transfers between devices with their start and end apart: 1, of which 1 were waited for; matrix products, arithmetic and copies ran while one was open for 0% of the time, Pallas kernels for 0%

profile of v1, /device:TPU:0, one launch (start us, length us, event | category | flops | bytes accessed | tf_op | source)
XLA Modules:
  0.0 214.1 jit_solution(3277085998214773750)
XLA Ops:
  0.0 1.6 convert_reduce_fusion.2
  1.7 1.8 multiply_reduce_fusion.1
  3.6 0.8 fusion.61
  4.5 1.8 fusion.42
  6.3 0.9 convolution_convert_fusion.2
  7.2 1.4 slice.48
  9.1 1.0 slice.49
  10.2 2.8 %collective-permute-done = bf16[1920,512]{1,0:T(8,128)(2,1)S(1)} collective-permute-done((bf16[1920,512]{1,0:T(8,128)(2,1)}, bf16[1920,512]{1,0:T(8,128)(2,1)S(1)}, u32[]{:S(2)}, u32[]{:S(2)}) %collective-permute-start) | collective-permute-done | bytes 1966112 | tf_op jit(solution)/shard_map/ppermute | solution.py:11
  12.9 1.4 copy-done.2
  14.3 48.6 %while.10 = (s32[]{:T(128)}, bf16[4,480,256]{2,1,0:T(8,128)(2,1)}, bf16[4,480,512]{2,1,0:T(8,128)(2,1)}, bf16[4,480,256]{2,1,0:T(8,128)(2,1)}, s32[]{:T(128)}) while((s32[]{:T(128)}, bf16[4,480,256]{2,1,0:T(8,128)(2,1)}, bf16[4,480,512]{2,1,0:T(8,128)(2,1)}, bf16[4,480,256]{2,1,0:T(8,128)(2,1)}, s32[]{:T(128)}) %tuple.42), condition=%wide.region_5.6_spmd, body=%wide.region_2.5_spmd.sunk | while | flops 245268960 | bytes 20675140 | solution.py:69
  14.3 1.2 constant_dynamic-slice_fusion.4
  15.7 1.0 constant_dynamic-slice_fusion.5
  16.8 4.8 %fusion.92 = (f32[8,480]{1,0:T(8,128)S(1)}, f32[8,480,480]{1,2,0:T(8,128)}) fusion(bf16[480,8,32]{0,2,1:T(8,128)(2,1)S(1)} %bitcast.86, bf16[480,8,32]{0,2,1:T(8,128)(2,1)S(1)} %bitcast.89), kind=kOutput, calls=%fused_computation.74.clone.1 | convolution fusion | flops 123494880 | bytes 7879680 | tf_op jit(solution)/shard_map/while/body/eval_jaxpr/sub | solution.py:31
  21.6 4.0 %fusion.93 = bf16[8,32,480]{2,1,0:T(8,128)(2,1)S(1)} fusion(bf16[480,8,32]{0,2,1:T(8,128)(2,1)S(1)} %bitcast.88, f32[8,480,480]{1,2,0:T(8,128)} %get-tuple-element.105, f32[8,480]{1,0:T(8,128)S(1)} %get-tuple-element.106), kind=kOutput, calls=%fused_computation.7.clone.1 | convolution fusion | flops 121774080 | bytes 7879680 | tf_op jit(solution)/shard_map/while/body/eval_jaxpr/hqk,khd->qhd/dot_general | solution.py:33
  26.5 1.1 constant_dynamic-slice_fusion.4
  27.8 1.0 constant_dynamic-slice_fusion.5
  28.9 4.8 %fusion.92 = (f32[8,480]{1,0:T(8,128)S(1)}, f32[8,480,480]{1,2,0:T(8,128)}) fusion(bf16[480,8,32]{0,2,1:T(8,128)(2,1)S(1)} %bitcast.86, bf16[480,8,32]{0,2,1:T(8,128)(2,1)S(1)} %bitcast.89), kind=kOutput, calls=%fused_computation.74.clone.1 | convolution fusion | flops 123494880 | bytes 7879680 | tf_op jit(solution)/shard_map/while/body/eval_jaxpr/sub | solution.py:31
  33.7 4.0 %fusion.93 = bf16[8,32,480]{2,1,0:T(8,128)(2,1)S(1)} fusion(bf16[480,8,32]{0,2,1:T(8,128)(2,1)S(1)} %bitcast.88, f32[8,480,480]{1,2,0:T(8,128)} %get-tuple-element.105, f32[8,480]{1,0:T(8,128)S(1)} %get-tuple-element.106), kind=kOutput, calls=%fused_computation.7.clone.1 | convolution fusion | flops 121774080 | bytes 7879680 | tf_op jit(solution)/shard_map/while/body/eval_jaxpr/hqk,khd->qhd/dot_general | solution.py:33
  38.6 1.1 constant_dynamic-slice_fusion.4
  39.9 1.0 constant_dynamic-slice_fusion.5
  41.1 4.8 %fusion.92 = (f32[8,480]{1,0:T(8,128)S(1)}, f32[8,480,480]{1,2,0:T(8,128)}) fusion(bf16[480,8,32]{0,2,1:T(8,128)(2,1)S(1)} %bitcast.86, bf16[480,8,32]{0,2,1:T(8,128)(2,1)S(1)} %bitcast.89), kind=kOutput, calls=%fused_computation.74.clone.1 | convolution fusion | flops 123494880 | bytes 7879680 | tf_op jit(solution)/shard_map/while/body/eval_jaxpr/sub | solution.py:31
  45.9 4.0 %fusion.93 = bf16[8,32,480]{2,1,0:T(8,128)(2,1)S(1)} fusion(bf16[480,8,32]{0,2,1:T(8,128)(2,1)S(1)} %bitcast.88, f32[8,480,480]{1,2,0:T(8,128)} %get-tuple-element.105, f32[8,480]{1,0:T(8,128)S(1)} %get-tuple-element.106), kind=kOutput, calls=%fused_computation.7.clone.1 | convolution fusion | flops 121774080 | bytes 7879680 | tf_op jit(solution)/shard_map/while/body/eval_jaxpr/hqk,khd->qhd/dot_general | solution.py:33
  50.7 1.1 constant_dynamic-slice_fusion.4
  52.1 1.0 constant_dynamic-slice_fusion.5
  53.2 4.8 %fusion.92 = (f32[8,480]{1,0:T(8,128)S(1)}, f32[8,480,480]{1,2,0:T(8,128)}) fusion(bf16[480,8,32]{0,2,1:T(8,128)(2,1)S(1)} %bitcast.86, bf16[480,8,32]{0,2,1:T(8,128)(2,1)S(1)} %bitcast.89), kind=kOutput, calls=%fused_computation.74.clone.1 | convolution fusion | flops 123494880 | bytes 7879680 | tf_op jit(solution)/shard_map/while/body/eval_jaxpr/sub | solution.py:31
  58.0 4.0 %fusion.93 = bf16[8,32,480]{2,1,0:T(8,128)(2,1)S(1)} fusion(bf16[480,8,32]{0,2,1:T(8,128)(2,1)S(1)} %bitcast.88, f32[8,480,480]{1,2,0:T(8,128)} %get-tuple-element.105, f32[8,480]{1,0:T(8,128)S(1)} %get-tuple-element.106), kind=kOutput, calls=%fused_computation.7.clone.1 | convolution fusion | flops 121774080 | bytes 7879680 | tf_op jit(solution)/shard_map/while/body/eval_jaxpr/hqk,khd->qhd/dot_general | solution.py:33
  62.9 1.7 convert_reduce_fusion.1
  65.8 30.7 %all_to_all.14 = bf16[1,4,480,256]{3,2,0,1:T(8,128)(2,1)S(1)} all-to-all(bf16[1,4,480,256]{3,2,0,1:T(8,128)(2,1)S(1)} %bitcast.94), channel_id=1, replica_groups=mesh['clips'=2,'frame'=4,'rows'=2,'view'=2] {'frame'}, dimensions={1} | all-to-all | bytes 1966080 | tf_op jit(solution)/shard_map/all_to_all | solution.py:83
  96.5 0.9 convolution_convert_fusion.1
  97.4 1.6 fusion.60
  99.0 1.5 copy.85
  100.5 4.6 %copy.69 = bf16[4,480,8,32]{3,0,1,2:T(4,128)(2,1)} copy(bf16[4,480,8,32]{1,3,2,0:T(8,128)(2,1)S(1)} %bitcast.91) | data formatting | bytes 1966080 | tf_op jit(solution)/shard_map/reshape | solution.py:41
  105.6 4.5 %copy.70 = bf16[4,480,8,32]{3,0,1,2:T(4,128)(2,1)} copy(bf16[4,480,8,32]{1,3,2,0:T(8,128)(2,1)S(1)} %bitcast.92) | data formatting | bytes 1966080 | tf_op jit(solution)/shard_map/reshape | solution.py:40
  110.1 8.4 %fusion.62 = f32[8,480,4,4]{3,2,1,0:T(4,128)} fusion(bf16[4,480,8,32]{3,0,1,2:T(4,128)(2,1)} %copy.69, bf16[4,480,8,32]{3,0,1,2:T(4,128)(2,1)} %copy.70), kind=kOutput, calls=%fused_computation.78 | convolution fusion | flops 3932160 | bytes 2211840 | tf_op jit(solution)/shard_map/fnhd,gnhd->hfgn/dot_general | solution.py:43
  118.5 5.1 %copy.71 = f32[8,480,4,4]{1,0,2,3:T(8,128)S(1)} copy(f32[8,480,4,4]{3,2,1,0:T(4,128)} %fusion.62) | data formatting | bytes 491520 | tf_op jit(solution)/shard_map/fnhd,gnhd->hfgn/dot_general | solution.py:43
  123.7 7.4 %copy.73 = bf16[8,4,4,480]{2,1,0,3:T(4,128)(2,1)} copy(bf16[8,4,4,480]{3,0,2,1:T(8,128)(2,1)S(1)} %divide_convert_fusion.4) | data formatting | bytes 245760 | tf_op jit(solution)/shard_map/convert_element_type | solution.py:48
  131.2 1.5 copy.84
  132.6 4.7 %copy.72 = bf16[4,480,8,32]{3,0,2,1:T(4,128)(2,1)} copy(bf16[4,480,8,32]{1,3,2,0:T(8,128)(2,1)S(1)} %bitcast.93) | data formatting | bytes 1966080 | tf_op jit(solution)/shard_map/reshape | solution.py:42
  137.3 9.4 %fusion.20 = bf16[4,480,8,32]{3,0,2,1:T(4,128)(2,1)} fusion(bf16[4,480,8,32]{3,0,2,1:T(4,128)(2,1)} %copy.72, bf16[8,4,4,480]{2,1,0,3:T(4,128)(2,1)} %copy.73), kind=kOutput, calls=%fused_computation.24 | convolution fusion | flops 4423680 | bytes 2088960 | tf_op jit(solution)/shard_map/hfgn,gnhd->fnhd/dot_general | solution.py:49
  146.7 13.9 %fusion.59 = (bf16[1,480,8,32]{3,0,2,1:T(2,128)(2,1)}, bf16[1,480,8,32]{3,0,2,1:T(2,128)(2,1)}, bf16[1,480,8,32]{3,0,2,1:T(2,128)(2,1)}, bf16[1,480,8,32]{3,0,2,1:T(2,128)(2,1)}) fusion(bf16[4,480,8,32]{3,0,2,1:T(4,128)(2,1)} %fusion.20), kind=kLoop, calls=%fused_computation.75 | loop fusion | bytes 1966080 | tf_op jit(solution)/shard_map/split | solution.py:97
  160.6 4.4 %copy.74 = bf16[1,480,8,32]{1,3,2,0:T(8,128)(2,1)S(1)} copy(bf16[1,480,8,32]{3,0,2,1:T(2,128)(2,1)} %get-tuple-element.60) | data formatting | bytes 491520 | tf_op jit(solution)/shard_map/split | solution.py:97
  165.0 4.4 %copy.75 = bf16[1,480,8,32]{1,3,2,0:T(8,128)(2,1)S(1)} copy(bf16[1,480,8,32]{3,0,2,1:T(2,128)(2,1)} %get-tuple-element.63) | data formatting | bytes 491520 | tf_op jit(solution)/shard_map/split | solution.py:97
  169.4 4.4 %copy.76 = bf16[1,480,8,32]{1,3,2,0:T(8,128)(2,1)S(1)} copy(bf16[1,480,8,32]{3,0,2,1:T(2,128)(2,1)} %get-tuple-element.62) | data formatting | bytes 491520 | tf_op jit(solution)/shard_map/split | solution.py:97
  173.8 5.5 %copy.77 = bf16[1,480,8,32]{1,3,2,0:T(8,128)(2,1)} copy(bf16[1,480,8,32]{3,0,2,1:T(2,128)(2,1)} %get-tuple-element.61) | data formatting | bytes 491520 | tf_op jit(solution)/shard_map/split | solution.py:97
  179.4 1.1 pad_maximum_fusion
  181.0 26.9 %all_to_all.15 = bf16[4,1,1,480,256]{4,3,2,1,0:T(8,128)(2,1)S(1)} all-to-all(bf16[4,1,1,480,256]{4,3,2,1,0:T(8,128)(2,1)S(1)} %copy.78), channel_id=1, replica_groups=mesh['clips'=2,'frame'=4,'rows'=2,'view'=2] {'frame'}, dimensions={0} | all-to-all | bytes 1966080 | tf_op jit(solution)/shard_map/all_to_all | solution.py:96
  207.9 1.4 convert_reduce_fusion
  210.0 4.2 %fusion.27 = bf16[1920,256]{1,0:T(8,128)(2,1)} fusion(bf16[1024,256]{1,0:T(8,128)(2,1)S(1)} %copy-done, bf16[256,1024]{1,0:T(8,128)(2,1)S(1)} %copy-done.6, bf16[1920,256]{1,0:T(8,128)(2,1)S(1)} %get-tuple-element.73, f32[256]{0:T(256)S(1)} %bitcast.104, f32[1920]{0:T(1024)S(1)} %add_rsqrt_fusion, f32[1920]{0:T(1024)S(1)} %broadcast_multiply_fusion), kind=kOutput, calls=%fused_computation.37 | convolution fusion | flops 2034892800 | bytes 3031040 | tf_op jit(solution)/shard_map/dot_general | solution.py:111
  (51 shorter events, 8.7 us)
Async XLA Ops:
  0.0 209.9 %copy-start = (bf16[1024,256]{1,0:T(8,128)(2,1)S(1)}, bf16[1024,256]{1,0:T(8,128)(2,1)}, u32[]{:S(2)}) copy-start(bf16[1024,256]{1,0:T(8,128)(2,1)} %param.17) | copy-start | bytes 1572868
  0.0 6.2 %copy-start.3 = (bf16[256,768]{1,0:T(8,128)(2,1)S(1)}, bf16[256,768]{1,0:T(8,128)(2,1)}, u32[]{:S(2)}) copy-start(bf16[256,768]{1,0:T(8,128)(2,1)} %param.12) | copy-start | bytes 1179652
  8.6 4.3 %collective-permute-start = (bf16[1920,512]{1,0:T(8,128)(2,1)}, bf16[1920,512]{1,0:T(8,128)(2,1)S(1)}, u32[]{:S(2)}, u32[]{:S(2)}) collective-permute-start(bf16[1920,512]{1,0:T(8,128)(2,1)} %slice.48), channel_id=1, source_target_pairs={{0,1},{1,0},{2,3},{3,2},{4,5},{5,4},{6,7},{7,6},{8,9},{9,8},{10,11... | collective-permute-start | bytes 5898248 | tf_op jit(solution)/shard_map/ppermute | solution.py:11
  12.9 1.4 copy-start.2
  14.3 48.6 %copy-start.1 = (bf16[1,1,4,480,256]{4,3,2,1,0:T(8,128)(2,1)S(1)}, bf16[1,1,4,480,256]{4,3,2,1,0:T(8,128)(2,1)}, u32[]{:S(2)}) copy-start(bf16[1,1,4,480,256]{4,3,2,1,0:T(8,128)(2,1)} %param.10) | copy-start | bytes 2949124
  14.3 48.6 %copy-start.5 = (bf16[256,256]{1,0:T(8,128)(2,1)S(1)}, bf16[256,256]{1,0:T(8,128)(2,1)}, u32[]{:S(2)}) copy-start(bf16[256,256]{1,0:T(8,128)(2,1)} %param.13) | copy-start | bytes 393220
  64.6 31.9 %copy-start.4 = (bf16[256,768]{1,0:T(8,128)(2,1)S(1)}, bf16[256,768]{1,0:T(8,128)(2,1)}, u32[]{:S(2)}) copy-start(bf16[256,768]{1,0:T(8,128)(2,1)} %param.14) | copy-start | bytes 1179652
  181.0 29.0 %copy-start.6 = (bf16[256,1024]{1,0:T(8,128)(2,1)S(1)}, bf16[256,1024]{1,0:T(8,128)(2,1)}, u32[]{:S(2)}) copy-start(bf16[256,1024]{1,0:T(8,128)(2,1)} %param.16) | copy-start | bytes 1572868
